TPU v7x, 32 devices: a whole 2x2x4 slice. The times are simulated.
32 devices in a mesh: tok: 8 (over z, x), tp: 4 (over y, core).
Axes of the slice: x: 2, y: 2, z: 4, core: 2. Of those that a mesh axis runs over, the one named last changes fastest.
Arguments:
- tokens: bfloat16 [36928, 768], P('tok'), may hold values from -6 to 6
- slot_index: int32 [36928], P('tok'), may hold values from -1 to 18477, as said below
- segment: int32 [36928], P('tok'), may hold values from 0 to 3, as said below
- router: float32 [768], replicated, may hold values from -0.21875 to 0.21875
- first_norm: float32 [2, 768], replicated, may hold values from -0.6 to 1.3
- qkv_weight: bfloat16 [768, 3, 768], P(None, None, 'tp'), may hold values from -0.21875 to 0.21875
- qv_bias: float32 [2, 768], P(None, 'tp'), may hold values from -4 to 4
- out_weight: bfloat16 [768, 768], P('tp'), may hold values from -1.75 to 1.75
- out_bias: float32 [768], P('tp'), may hold values from -4 to 4
- second_norm: float32 [2, 768], replicated, may hold values from -0.6 to 1.3
- up_weight: bfloat16 [768, 3072], P(None, 'tp'), may hold values from -0.21875 to 0.21875
- up_bias: float32 [3072], P('tp'), may hold values from -4 to 4
- down_weight: bfloat16 [3072, 768], P('tp'), may hold values from -0.109375 to 0.109375
- down_bias: float32 [768], P('tp'), may hold values from -4 to 4
- cotangent: bfloat16 [36928, 768], P('tok'), may hold values from -6 to 6
Outputs:
- layer_out: bfloat16 [36928, 768], P('tok', 'tp')
- d_tokens: float32 [36928, 768], P('tok', 'tp')
- d_qkv_weight: float32 [768, 3, 768], P(None, None, 'tp')
- d_qv_bias: float32 [2, 768], P(None, 'tp')
- d_out_weight: float32 [768, 768], P('tp')
- d_out_bias: float32 [768], P('tp')
- d_up_weight: float32 [768, 3072], P(None, 'tp')
- d_up_bias: float32 [3072], P('tp')
- d_down_weight: float32 [3072, 768], P('tp')
- d_down_bias: float32 [768], P('tp')
- d_first_norm: float32 [2, 768], P(None, 'tp')
- d_second_norm: float32 [2, 768], P(None, 'tp')
- d_router: float32 [768], P('tp')
Inputs may be any that keep to these rules, and one draw needn't show every extreme that they name: `slot_index`: -1 where the router leaves a patch out; else a slot of the compact buffers, slot // 289 being its row buffer, owned by index slot // 2312 of tok. No slot is named twice, each buffer's named slots are its lowest ones, every index of tok holds exactly 2168 selected patches and owns 2168 named slots, and at most 271 of the selected patches of one index of tok lie in rows of one owner. `segment`: within a row buffer the segments of named slots never fall from one slot to the next.
All inputs are finite; a program needn't handle non-finite values.
Results may differ from a plain program's by a relative error of at most 0.013.
Values may be sent and summed in bfloat16 or wider, within the bound.
No kernel may reach another device: no remote copies, remote signals or barrier semaphores. Data moves between devices by JAX's collectives and lax.ppermute only.
A program may use at most 320 MiB of HBM per device.

v0:
```python
import jax
import jax.numpy as jnp
from jax import lax
from jax.sharding import PartitionSpec as P

HD = 64
ROWS_DEV = 8
SLOTS = 289
EPSILON = 1e-06
MASKED_SCORE = -1000000000.0
BF = jnp.bfloat16
F32 = jnp.float32
EXACT = lax.Precision.HIGHEST


def ceil_to(value, step):
    return -(-value // step) * step


def normal_parts(values):
    row_mean = jnp.mean(values, axis=-1, keepdims=True)
    centered = values - row_mean
    inverse = lax.rsqrt(jnp.mean(centered * centered, axis=-1, keepdims=True) + EPSILON)
    return (centered * inverse, inverse)


def norm_back(grad_in, normal, inverse, gain_row):
    scaled = grad_in * gain_row
    return inverse * (
        scaled
        - jnp.mean(scaled, axis=-1, keepdims=True)
        - normal * jnp.mean(scaled * normal, axis=-1, keepdims=True)
    )


def mul(left, right):
    return lax.dot_general(left, right, (((1,), (0,)), ((), ())), preferred_element_type=F32)


def mul_t0(left, right):
    return lax.dot_general(left, right, (((0,), (0,)), ((), ())), preferred_element_type=F32)


def mul_t1(left, right):
    return lax.dot_general(left, right, (((1,), (1,)), ((), ())), preferred_element_type=F32)


def hot(rows, cols):
    return (rows[:, None] == cols[None, :]).astype(BF)


def columns_of(source, part, shares):
    width = source.shape[-1] // shares
    return lax.dynamic_slice_in_dim(source, part * width, width, source.ndim - 1)


def body(
    tokens,
    slot_index,
    segment,
    router,
    first_norm,
    qkv_weight,
    qv_bias,
    out_weight,
    out_bias,
    second_norm,
    up_weight,
    up_bias,
    down_weight,
    down_bias,
    cotangent,
):
    peers = lax.axis_size("tok")
    shares = lax.axis_size("tp")
    part = lax.axis_index("tp")
    half_bit = part % 2
    pair_bit = part // 2
    half_swap = [(i, i ^ 1) for i in range(shares)]
    pair_swap = [(i, i ^ 2) for i in range(shares)]
    count, width = tokens.shape
    inner = qkv_weight.shape[2]
    heads_local = inner // HD
    owned = ROWS_DEV * SLOTS
    live = owned - owned // 16
    capacity = -(-live // peers)
    quarter = -(-capacity // shares)
    block = ceil_to(quarter + 1, 8)
    picked = peers * block
    idle_share = -(-(count - live) // shares)
    idle = ceil_to(idle_share, 16)
    own = picked + idle
    chosen = slot_index >= 0
    owner = jnp.where(chosen, slot_index // owned, peers)
    lanes = jnp.arange(peers, dtype=jnp.int32)
    match = (owner[:, None] == lanes[None, :]).astype(jnp.int32)
    rank = jnp.sum(jnp.cumsum(match, axis=0) * match, axis=1) - 1
    idle_rank = jnp.cumsum(jnp.where(chosen, 0, 1)) - 1
    piece = rank // quarter
    offset = rank % quarter
    mine = chosen & (piece % 2 == half_bit)
    far = piece // 2 ^ pair_bit
    send_row = jnp.where(mine, (owner * 2 + far) * block + offset, -1)
    picked_row = jnp.where(mine & (far == 0), owner * block + offset, -1)
    own_row = jnp.where(
        chosen,
        picked_row,
        jnp.where(idle_rank // idle_share == part, picked + idle_rank % idle_share, -1),
    )
    back_picked = jnp.where(chosen, piece * picked + owner * block + offset, -1)
    back_idle = jnp.where(chosen, -1, idle_rank // idle_share * idle + idle_rank % idle_share)
    up_all = lax.all_gather(up_weight, "tp")
    down_all = lax.all_gather(down_weight, "tp")
    send_hot = hot(jnp.arange(2 * picked, dtype=jnp.int32), send_row)
    own_hot = hot(jnp.arange(own, dtype=jnp.int32), own_row)
    send_in = mul(send_hot, tokens)
    send_hat, _ = normal_parts(send_in)
    send_rows = (send_hat * first_norm[0] + first_norm[1]).astype(BF)
    local_slot = jnp.where(chosen, slot_index % owned, 0)
    marks = jnp.stack([local_slot // 64 + 1, local_slot % 64, segment])
    block_of = jnp.where(mine, owner * 2 + far, -1)
    block_hot = jnp.arange(2 * peers, dtype=jnp.int32)[:, None] == block_of[None, :]
    mark_left = jnp.where(block_hot[None], marks[:, None, :], 0).astype(BF)
    mark_right = hot(offset, jnp.arange(128, dtype=jnp.int32))
    mark_rows = mul(mark_left.reshape(6 * peers, count), mark_right).astype(BF)
    mark_rows = mark_rows.reshape(3, 2 * peers, 128).transpose(1, 0, 2).reshape(2 * peers, 1, 384)
    mark_rows = jnp.pad(mark_rows, ((0, 0), (0, 0), (0, width - 384)))
    row_kind = jnp.arange(block, dtype=jnp.int32)[None, :, None] == quarter
    send_rows = jnp.where(row_kind, mark_rows, send_rows.reshape(2 * peers, block, width))
    got_near = lax.all_to_all(
        send_rows.reshape(peers, 2, block, width), "tok", split_axis=0, concat_axis=0, tiled=True
    )
    got_far = lax.ppermute(got_near, "tp", half_swap)
    got = jnp.stack([got_near, got_far])
    mark = got[:, :, :, quarter, :].astype(jnp.int32)
    recv_slot = (mark[..., 0:block] - 1) * 64 + mark[..., 128 : 128 + block]
    recv_segment = mark[..., 256 : 256 + block]
    slot_rows = recv_slot.transpose(0, 2, 1, 3).reshape(4 * picked)
    segment_rows = recv_segment.transpose(0, 2, 1, 3).reshape(4 * picked)
    features = got.transpose(0, 2, 1, 3, 4).reshape(4 * picked, width)
    pad = 304
    ids = jnp.arange(ROWS_DEV * pad, dtype=jnp.int32)
    slot_ids = jnp.where(ids % pad < SLOTS, ids // pad * SLOTS + ids % pad, -1000)
    slot_hot = hot(slot_ids, slot_rows)
    slot_features = mul(slot_hot, features).astype(BF)
    flat_weight = qkv_weight.reshape(width, 3 * inner)
    bias_row = jnp.concatenate([qv_bias[0], jnp.zeros_like(qv_bias[0]), qv_bias[1]])
    slot_qkv = (mul(slot_features, flat_weight) + bias_row).astype(BF)
    slot_segment = (
        jnp.sum(jnp.where(slot_hot > 0, segment_rows[None, :] + 1, 0), axis=1) - 1
    ).reshape(ROWS_DEV, pad)
    allowed = (slot_segment[:, :, None] == slot_segment[:, None, :]) & (
        slot_segment[:, None, :] >= 0
    )
    grouped = slot_qkv.reshape(ROWS_DEV, pad, 3, heads_local, HD)
    query, key, value = (grouped[:, :, 0], grouped[:, :, 1], grouped[:, :, 2])
    score_scale = HD ** (-0.5)
    scores = jnp.einsum("rqhe,rkhe->rhqk", query, key, preferred_element_type=F32) * score_scale
    scores = jnp.where(allowed[:, None], scores, MASKED_SCORE)
    top = jnp.max(scores, axis=-1, keepdims=True)
    raised = jnp.exp(scores - top)
    weights = raised / jnp.sum(raised, axis=-1, keepdims=True)
    weights_low = weights.astype(BF)
    attended = jnp.einsum("rhqk,rkhe->rqhe", weights_low, value, preferred_element_type=F32)
    heads = attended.reshape(ROWS_DEV * pad, inner).astype(BF)
    heads_rows = mul_t0(slot_hot, heads).astype(BF)
    bias_full = lax.dynamic_update_slice(
        jnp.zeros((width,), F32), out_bias, (part * (width // shares),)
    )

    def share_sum(partial):
        near, far_half = (partial[: 2 * picked], partial[2 * picked :])
        got_half = lax.ppermute(far_half.astype(BF), "tp", half_swap)
        joined = near + got_half.astype(F32)
        got_pair = lax.ppermute(joined[picked:].astype(BF), "tp", pair_swap)
        return (joined[:picked] + got_pair.astype(F32)).astype(BF)

    def across(rows):
        return lax.all_to_all(
            rows.reshape(peers, block, width), "tok", split_axis=0, concat_axis=0, tiled=True
        ).reshape(picked, width)

    returned = across(share_sum(mul(heads_rows, out_weight) + bias_full))
    own_in = mul(own_hot, tokens)
    own_cot_low = mul(own_hot, cotangent).astype(BF)
    own_cot = own_cot_low.astype(F32)
    gate = jax.nn.sigmoid(jnp.dot(own_in, router, precision=EXACT))
    branch = jnp.pad(returned.astype(F32), ((0, idle), (0, 0)))
    scale = jnp.where(jnp.arange(own) < picked, gate, 0.0)
    residual = own_in + scale[:, None] * branch
    second_hat, second_inv = normal_parts(residual)
    second = (second_hat * second_norm[0] + second_norm[1]).astype(BF)
    up_cols = up_all.transpose(1, 0, 2).reshape(width, -1)
    down_rows = down_all.reshape(-1, width)
    up_bias_all = lax.all_gather(up_bias, "tp", tiled=True)
    down_bias_all = lax.all_gather(down_bias, "tp", tiled=True)
    pre = mul(second, up_cols) + up_bias_all
    below = 0.5 * (1.0 + lax.erf(pre * 2.0 ** (-0.5)))
    bell = jnp.exp(-0.5 * pre * pre) * (2.0 * jnp.pi) ** (-0.5)
    hidden = (pre * below).astype(BF)
    layer_rows = (residual + mul(hidden, down_rows) + down_bias_all).astype(BF)
    d_hidden = mul_t1(own_cot_low, down_rows)
    d_pre = (d_hidden * (below + pre * bell)).astype(BF)
    d_down = mul_t0(hidden, own_cot_low).astype(BF).reshape(shares, -1, width)
    d_up = mul_t0(second, d_pre).astype(BF)
    d_up = d_up.reshape(width, shares, -1).transpose(1, 0, 2)
    d_second = mul_t1(d_pre, up_cols)
    d_residual = own_cot + norm_back(d_second, second_hat, second_inv, second_norm[0])
    d_branch = (d_residual[:picked] * scale[:picked, None]).astype(BF)
    d_logit = jnp.sum(d_residual * branch, axis=1) * scale * (1.0 - gate)
    small = jnp.concatenate(
        [
            jnp.sum(d_pre.astype(F32), axis=0).reshape(shares, width),
            jnp.stack(
                [
                    jnp.sum(d_second * second_hat, axis=0),
                    jnp.sum(d_second, axis=0),
                    jnp.sum(own_cot, axis=0),
                    jnp.sum(d_branch.astype(F32), axis=0),
                    jnp.sum(d_logit[:, None] * own_in, axis=0),
                ]
            ),
        ]
    )
    d_up_share = lax.psum_scatter(d_up, "tp", scatter_dimension=0)
    d_down_share = lax.psum_scatter(d_down, "tp", scatter_dimension=0)
    d_up_total = lax.psum(d_up_share, "tok").astype(F32)
    d_down_total = lax.psum(d_down_share, "tok").astype(F32)
    grad_own = across(d_branch)
    grad_near = jnp.concatenate([grad_own, lax.ppermute(grad_own, "tp", pair_swap)])
    grad_rows = jnp.concatenate([grad_near, lax.ppermute(grad_near, "tp", half_swap)])
    d_out_weight = mul_t0(heads_rows, grad_rows)
    d_heads_rows = mul_t1(grad_rows, out_weight).astype(BF)
    d_heads = mul(slot_hot, d_heads_rows).astype(BF).reshape(ROWS_DEV, pad, heads_local, HD)
    d_weights = jnp.einsum("rqhe,rkhe->rhqk", d_heads, value, preferred_element_type=F32)
    d_value = jnp.einsum("rhqk,rqhe->rkhe", weights_low, d_heads, preferred_element_type=F32)
    d_scores = (
        weights * (d_weights - jnp.sum(weights * d_weights, axis=-1, keepdims=True))
    ).astype(BF)
    d_query = jnp.einsum("rhqk,rkhe->rqhe", d_scores, key, preferred_element_type=F32) * score_scale
    d_key = jnp.einsum("rhqk,rqhe->rkhe", d_scores, query, preferred_element_type=F32) * score_scale
    d_qkv = (
        jnp.stack([d_query, d_key, d_value], axis=2).astype(BF).reshape(ROWS_DEV * pad, 3 * inner)
    )
    d_qkv_weight = mul_t0(slot_features, d_qkv)
    d_qkv_bias = jnp.sum(d_qkv.astype(F32), axis=0).reshape(3, inner)
    d_qv_bias = jnp.stack([d_qkv_bias[0], d_qkv_bias[2]])
    d_qkv_rows = mul_t0(slot_hot, d_qkv).astype(BF)
    d_normed = across(share_sum(mul_t1(d_qkv_rows, flat_weight))).astype(F32)
    d_qkv_total = lax.psum(d_qkv_weight.astype(BF), "tok").astype(F32)
    d_out_total = lax.psum(d_out_weight.astype(BF), "tok").astype(F32)
    first_hat, first_inv = normal_parts(own_in[:picked])
    d_picked = (
        d_residual[:picked]
        + norm_back(d_normed, first_hat, first_inv, first_norm[0])
        + d_logit[:picked, None] * router[None, :]
    ).astype(BF)
    d_idle = d_residual[picked:].astype(BF)

    def to_columns(rows):
        pieces = rows.reshape(rows.shape[0], shares, width // shares).transpose(1, 0, 2)
        return lax.all_to_all(pieces, "tp", split_axis=0, concat_axis=0, tiled=True).reshape(
            shares * rows.shape[0], width // shares
        )

    picked_hot = hot(back_picked, jnp.arange(shares * picked, dtype=jnp.int32))
    idle_hot = hot(back_idle, jnp.arange(shares * idle, dtype=jnp.int32))
    layer_out = (
        mul(picked_hot, to_columns(layer_rows[:picked]))
        + mul(idle_hot, to_columns(layer_rows[picked:]))
    ).astype(BF)
    d_tokens = mul(picked_hot, to_columns(d_picked)) + mul(idle_hot, to_columns(d_idle))
    first_pair = jnp.stack([jnp.sum(d_normed * first_hat, axis=0), jnp.sum(d_normed, axis=0)])
    small = lax.psum(jnp.concatenate([small, first_pair]), ("tok", "tp"))
    small_cols = columns_of(small[shares:], part, shares)
    d_up_bias = lax.dynamic_slice_in_dim(small, part, 1, 0).reshape(width)
    d_qv_bias = lax.psum(d_qv_bias, "tok")
    return (
        layer_out,
        d_tokens,
        d_qkv_total.reshape(width, 3, inner),
        d_qv_bias,
        d_out_total,
        small_cols[3],
        d_up_total,
        d_up_bias,
        d_down_total,
        small_cols[2],
        small_cols[5:7],
        small_cols[0:2],
        small_cols[4],
    )


def solution(mesh):
    return jax.shard_map(
        body,
        mesh=mesh,
        in_specs=(
            P("tok", None),
            P("tok"),
            P("tok"),
            P(),
            P(),
            P(None, None, "tp"),
            P(None, "tp"),
            P("tp", None),
            P("tp"),
            P(),
            P(None, "tp"),
            P("tp"),
            P("tp", None),
            P("tp"),
            P("tok", None),
        ),
        out_specs=(
            P("tok", "tp"),
            P("tok", "tp"),
            P(None, None, "tp"),
            P(None, "tp"),
            P("tp", None),
            P("tp"),
            P(None, "tp"),
            P("tp"),
            P("tp", None),
            P("tp"),
            P(None, "tp"),
            P(None, "tp"),
            P("tp"),
        ),
        check_vma=False,
    )
```

profile of v0, /device:TPU:0, one launch (start us, length us, event | category | flops | bytes accessed | tf_op | source)
XLA Modules:
  0.0 696.7 jit_solution(4545855774942127467)
XLA Ops:
  16.0 14.7 %fusion.135 = (f32[1152]{0:T(1024)S(1)}, f32[1152,768]{1,0:T(8,128)S(1)}) fusion(bf16[4616,768]{1,0:T(8,128)(2,1)} %param.15, s32[4616]{0:T(1024)S(1)} %get-tuple-element.46), kind=kOutput, calls=%fused_computation.269 | convolution fusion | flops 8174084096 | bytes 10652192 | tf_op jit(solution)/shard_map/dot_general | solution.py:37
  32.1 48.4 %all_to_all.40 = bf16[8,2,72,768]{3,2,1,0:T(8,128)(2,1)S(1)} all-to-all(bf16[8,2,72,768]{3,2,1,0:T(8,128)(2,1)S(1)} %broadcast_select_fusion), channel_id=1, replica_groups=mesh['tok'=8,'tp'=4] {'tok'}, dimensions={0} | all-to-all | bytes 3538944 | tf_op jit(solution)/shard_map/all_to_all | solution.py:130
  85.6 3.9 pad_maximum_fusion
  89.7 12.9 %fusion.44 = bf16[2432,768]{1,0:T(8,128)(2,1)} fusion(bf16[2304,768]{1,0:T(8,128)(2,1)} %bitcast.217, s32[2304]{0:T(1024)S(1)} %eq.201, s32[2432]{0:T(1024)S(1)} %fusion.120), kind=kOutput, calls=%fused_computation.64 | convolution fusion | flops 8614182912 | bytes 7293440 | tf_op jit(solution)/shard_map/dot_general | solution.py:37
  102.6 3.8 select_reduce_fusion
  106.5 6.2 add_convert_fusion
  112.7 7.5 %reshape.344 = bf16[8,304,3,3,64]{1,0,4,3,2:T(8,128)(2,1)} reshape(bf16[2432,576]{0,1:T(8,128)(2,1)} %add_convert_fusion) | data formatting | bytes 5603328 | tf_op jit(solution)/shard_map/reshape | solution.py:155
  125.7 8.3 %fusion.136 = (f32[8,3,304]{2,1,0:T(4,128)S(1)}, f32[8,3,304,304]{2,3,1,0:T(8,128)}) fusion(pred[8,304,304]{1,2,0:T(8,128)(4,1)} %compare_and_fusion, bf16[8,304,1,3,64]{1,0,4,3,2:T(8,128)(2,1)S(1)} %get-tuple-element.38, bf16[8,304,1,3,64]{1,0,4,3,2:T(8,128)(2,1)S(1)} %get-tuple-element.37), kind=kOutput, calls=%fused_computation.270 | convolution fusion | flops 292774176 | bytes 11508224 | tf_op jit(solution)/shard_map/sub | solution.py:161
  134.0 5.8 fusion.83
  141.4 4.1 fusion.53
  150.0 3.7 collective-permute-done.1
  158.5 15.1 %fusion.16 = f32[1200,768]{1,0:T(8,128)S(1)} fusion(bf16[4616,768]{1,0:T(8,128)(2,1)} %param.15, s32[4616]{0:T(1024)S(1)} %get-tuple-element.47), kind=kOutput, calls=%fused_computation.20 | convolution fusion | flops 8513750528 | bytes 10795040 | tf_op jit(solution)/shard_map/dot_general | solution.py:37
  178.8 20.2 %all-gather.2 = f32[4,1,768]{2,1,0:T(1,128)S(1)} all-gather(f32[1,1,768]{2,1,0:T(1,128)S(1)} %reshape.375), channel_id=1, replica_groups=mesh['tok'=8,'tp'=4] {'tp'}, dimensions={0}, use_global_device_ids=true | all-gather | bytes 15360 | tf_op jit(solution)/shard_map/all_gather | solution.py:195
  200.2 3.6 all-to-all-start.1
  203.8 14.8 %fusion.65 = bf16[1200,768]{1,0:T(8,128)(2,1)} fusion(bf16[4616,768]{1,0:T(8,128)(2,1)} %param.29, s32[4616]{0:T(1024)S(1)} %get-tuple-element.47), kind=kOutput, calls=%fused_computation.100 | convolution fusion | flops 8514672128 | bytes 8951840 | tf_op jit(solution)/shard_map/dot_general | solution.py:37
  218.6 6.6 copy.121
  231.2 10.5 %multiply_convert_fusion = (bf16[1200,3072]{1,0:T(8,128)(2,1)S(1)}, f32[1200,3072]{1,0:T(8,128)}) fusion(f32[3072]{0:T(1024)S(1)} %bitcast.228, bf16[768,3072]{0,1:T(8,128)(2,1)S(1)} %bitcast.209, f32[768]{0:T(1024)S(1)} %get-tuple-element.24, f32[768]{0:T(1024)S(1)} %get-tuple-element.23, f32[1200]{0:T(1024)S(1)} %add_rsqrt_fusion, ...), kind=kOutput, calls=%fused_computation.34 | convolution fusion | flops 5691801600 | bytes 31440960 | tf_op jit(solution)/shard_map/dot_general | solution.py:37
  241.7 8.3 %convolution_convert_fusion = bf16[3072,768]{1,0:T(8,128)(2,1)} fusion(bf16[1200,3072]{1,0:T(8,128)(2,1)S(1)} %get-tuple-element.67, bf16[1200,768]{1,0:T(8,128)(2,1)S(1)} %copy-done.16), kind=kOutput, calls=%fused_computation.65 | convolution fusion | flops 5664669696 | bytes 13934592 | tf_op jit(solution)/shard_map/dot_general | solution.py:41
  250.2 14.4 %convert_reduce_fusion = (f32[3072]{0:T(1024)}, bf16[1200,3072]{1,0:T(8,128)(2,1)S(1)}) fusion(f32[1200,3072]{1,0:T(8,128)} %get-tuple-element.68, bf16[1200,768]{1,0:T(8,128)(2,1)} %fusion.65, bf16[3072,768]{1,0:T(8,128)(2,1)} %all-gather.8.cloned.1.call-done), kind=kOutput, calls=%fused_computation.33 | convolution fusion | flops 5706544128 | bytes 28692480 | tf_op jit(solution)/shard_map/dot_general | solution.py:45
  264.6 13.4 %multiply_reduce_fusion.2 = (f32[768]{0:T(1024)}, f32[1200]{0:T(1024)S(1)}, f32[1200]{0:T(1024)S(1)}, f32[768]{0:T(1024)}, f32[1200,768]{1,0:T(8,128)S(1)}) fusion(f32[1200]{0:T(1024)S(1)} %add_rsqrt_fusion, f32[1200]{0:T(1024)S(1)} %broadcast_multiply_fusion.2, f32[1200,768]{1,0:T(8,128)S(1)} %copy-done.3, bf16[576,768]{1,0:T(8,128)(2,1)S(1)} %bitcast.199, ...), kind=kOutput, calls=%fused_computation.86 | convolution fusion | flops 5673365504 | bytes 20382144 | tf_op jit(solution)/shard_map/dot_general | solution.py:45
  278.0 4.2 fusion.60
  284.8 27.2 %all_to_all.41 = bf16[8,72,768]{2,1,0:T(8,128)(2,1)S(1)} all-to-all(bf16[8,72,768]{2,1,0:T(8,128)(2,1)S(1)} %bitcast.218), channel_id=1, replica_groups=mesh['tok'=8,'tp'=4] {'tok'}, dimensions={0} | all-to-all | bytes 1769472 | tf_op jit(solution)/shard_map/all_to_all | solution.py:179
  317.4 17.7 %all-reduce.4 = f32[768]{0:T(1024)} all-reduce(f32[768]{0:T(1024)} %dynamic-update-slice), channel_id=1, replica_groups=mesh['tok'=8,'tp'=4] {'tp'}, use_global_device_ids=true, to_apply=%add.4 | all-reduce | flops 768 | bytes 6144
  336.6 10.9 %convolution_convert_fusion.1 = bf16[768,3072]{1,0:T(8,128)(2,1)S(1)} fusion(bf16[1200,3072]{1,0:T(8,128)(2,1)} %copy-done.52, f32[768]{0:T(1024)} %copy-done.45, f32[768]{0:T(1024)} %copy-done.34, f32[1200]{0:T(1024)} %copy-done.31, f32[1200]{0:T(1024)S(1)} %broadcast_multiply_fusion.2, f32[1200,768]{1,0:T(8,128)} %copy-done.1, ...), kind=kOutput, calls=%fused_computation.66 | convolution fusion | flops 5672042496 | bytes 16683072 | tf_op jit(solution)/shard_map/dot_general | solution.py:41
  350.0 7.7 %fusion.56 = bf16[2432,192]{0,1:T(8,128)(2,1)} fusion(s32[2304]{0:T(1024)} %copy-done.39, s32[2432]{0:T(1024)} %copy-done.41, bf16[192,768]{1,0:T(8,128)(2,1)} %param.22, bf16[1152,768]{1,0:T(8,128)(2,1)} %collective-permute-done.4, bf16[576,768]{1,0:T(8,128)(2,1)S(1)} %collective-permute-done.3, bf16[576,768]{1,0:T(8,128)(2,1)S(1)} %bitcast.214), kind=kOutput, calls=%fused_computation.81 | convolution fusion | flops 2848284672 | bytes 4786688 | tf_op jit(solution)/shard_map/dot_general | solution.py:37
  360.5 6.4 fusion.75
  366.8 8.9 %multiply_reduce_fusion = (f32[8,3,304]{2,1,0:T(4,128)S(1)}, f32[8,3,304,304]{2,3,1,0:T(8,128)}) fusion(f32[8,3,304,304]{2,3,1,0:T(8,128)} %get-tuple-element.66, f32[8,3,304]{2,1,0:T(4,128)S(1)} %copy-done.29, bf16[8,304,1,3,64]{1,0,4,3,2:T(8,128)(2,1)S(1)} %copy-done.18, bf16[8,304,3,64]{1,0,3,2:T(8,128)(2,1)S(1)} %reshape.354), kind=kOutput, calls=%fused_computation.40 | convolution fusion | flops 290548608 | bytes 19670016 | tf_op jit(solution)/shard_map/rqhe,rkhe->rhqk/dot_general | solution.py:235
  375.8 6.1 multiply_convert_fusion.1
  386.1 4.1 copy.131
  390.2 6.7 convert_element_type.200
  396.9 16.6 %fusion.62 = f32[2304,768]{1,0:T(8,128)} fusion(bf16[768,576]{0,1:T(8,128)(2,1)S(1)} %bitcast.192, bf16[2432,576]{0,1:T(8,128)(2,1)} %convert_element_type.200, s32[2304]{0:T(1024)S(1)} %copy-done.40, s32[2432]{0:T(1024)S(1)} %copy-done.42), kind=kOutput, calls=%fused_computation.98 | convolution fusion | flops 8500396032 | bytes 10783232 | tf_op jit(solution)/shard_map/dot_general | solution.py:45
  413.6 3.8 slice.288
  417.8 10.6 %fusion.64 = bf16[1200,768]{1,0:T(8,128)(2,1)S(1)} fusion(bf16[1200,3072]{1,0:T(8,128)(2,1)} %copy-done.54, bf16[3072,768]{1,0:T(8,128)(2,1)} %all-gather.8.cloned.1.call-done, f32[768]{0:T(1024)S(1)} %copy-done.49, f32[1200,768]{1,0:T(8,128)} %copy-done.1, bf16[576,768]{1,0:T(8,128)(2,1)S(1)} %bitcast.202, f32[1200]{0:T(1024)S(1)} %fusion.123), kind=kOutput, calls=%fused_computation.99 | convolution fusion | flops 5667840000 | bytes 18513600 | tf_op jit(solution)/shard_map/dot_general | solution.py:37
  437.6 10.7 %all-to-all-done.2 = bf16[4,576,192]{1,2,0:T(8,128)(2,1)S(1)} async-done(((bf16[4,576,192]{1,2,0:T(8,128)(2,1)}), bf16[4,576,192]{1,2,0:T(8,128)(2,1)S(1)}, u32[]{:S(2)}, u32[]{:S(2)}) %all-to-all-start.2) | async-done | bytes 884768 | tf_op jit(solution)/shard_map/all_to_all | solution.py:262
  448.2 4.2 all-to-all-start.3
  462.2 4.1 all-to-all-done.3
  466.3 3.5 all-to-all-start.7
  483.0 13.4 %fusion.2 = f32[4616,192]{0,1:T(8,128)} fusion(bf16[2496,192]{0,1:T(8,128)(2,1)} %reshape.351, s32[4616]{0:T(1024)S(1)} %copy-done.33), kind=kOutput, calls=%fused_computation.3 | convolution fusion | flops 4435791360 | bytes 4522016 | tf_op jit(solution)/shard_map/dot_general | solution.py:37
  496.5 6.8 collective-permute-done.6
  505.9 4.7 all-to-all-start.5
  510.6 13.9 %fusion.40 = bf16[4616,192]{0,1:T(8,128)(2,1)} fusion(f32[4616,192]{0,1:T(8,128)} %fusion.2, bf16[2304,192]{0,1:T(8,128)(2,1)} %reshape.349, s32[4616]{0:T(1024)S(1)} %copy-done.32), kind=kOutput, calls=%fused_computation.57 | convolution fusion | flops 4096349184 | bytes 6220832 | tf_op jit(solution)/shard_map/dot_general | solution.py:37
  529.0 4.0 fusion.86
  543.3 3.7 all-to-all-start.6
  547.0 13.5 %fusion.1 = f32[4616,192]{0,1:T(8,128)} fusion(bf16[2496,192]{0,1:T(8,128)(2,1)} %reshape.359, s32[4616]{0:T(1024)S(1)} %copy-done.33), kind=kOutput, calls=%fused_computation.2 | convolution fusion | flops 4435791360 | bytes 4522016 | tf_op jit(solution)/shard_map/dot_general | solution.py:37
  560.7 23.7 %psum.43 = f32[2,192]{1,0:T(2,128)} all-reduce(f32[2,192]{1,0:T(2,128)S(1)} %pad_maximum_fusion.8), channel_id=1, replica_groups=mesh['tok'=8,'tp'=4] {'tok'}, use_global_device_ids=true, to_apply=%region_22.23 | all-reduce | flops 384 | bytes 3072 | tf_op jit(solution)/shard_map/psum | solution.py:277
  584.4 38.3 %psum.45 = f32[11,768]{1,0:T(8,128)S(1)} all-reduce(f32[11,768]{1,0:T(8,128)S(1)} %concatenate.16), channel_id=1, replica_groups=mesh['tok'=8,'tp'=4] {'tok','tp'}, use_global_device_ids=true, to_apply=%region_32.33 | all-reduce | flops 8448 | bytes 67584 | tf_op jit(solution)/shard_map/psum | solution.py:274
  626.1 13.6 %fusion.39 = f32[4616,192]{0,1:T(8,128)} fusion(f32[4616,192]{0,1:T(8,128)} %fusion.1, bf16[2304,192]{0,1:T(8,128)(2,1)S(1)} %reshape.357, s32[4616]{0:T(1024)S(1)} %copy-done.32), kind=kOutput, calls=%fused_computation.56 | convolution fusion | flops 4095462912 | bytes 7993376 | tf_op jit(solution)/shard_map/dot_general | solution.py:37
  639.7 42.5 %all-reduce.8.cloned.1.call-done = (bf16[768,3,192]{0,2,1:T(8,128)(2,1)}, bf16[192,768]{1,0:T(8,128)(2,1)}, bf16[768,768]{1,0:T(8,128)(2,1)}, bf16[768,768]{1,0:T(8,128)(2,1)}) async-done(((bf16[768,3,192]{0,2,1:T(8,128)(2,1)}, bf16[192,768]{1,0:T(8,128)(2,1)}, bf16[768,768]{1,0:T(8,128)(2,1)}, bf16[768,768]{1,0:T(8,128)(2,1)}), (bf16[768,3,192]{0,2,1:T(8,128)(2,1)}, bf16[192,768]{1,0:T(8,128)(2,1)}, ...) | async-done | bytes 3538960 | tf_op jit(solution)/shard_map/psum | solution.py:250
  (285 shorter events, 123.1 us)
Async XLA Ops:
  7.2 99.3 %copy-start = (bf16[768,3,192]{0,2,1:T(8,128)(2,1)S(1)}, bf16[768,3,192]{0,2,1:T(8,128)(2,1)}, u32[]{:S(2)}) copy-start(bf16[768,3,192]{0,2,1:T(8,128)(2,1)} %param.20) | copy-start | bytes 2654212
  7.2 211.4 %all-gather.6.cloned.1.call-start = ((), (), s32[]{:S(2)}) async-start(), calls=%async_computation.12 | async-start | bytes 5898240 | tf_op jit(solution)/shard_map/all_gather | solution.py:112
  8.1 23.2 %copy-start.23 = (f32[768]{0:T(1024)}, f32[768]{0:T(1024)S(1)}, u32[]{:S(2)}) copy-start(f32[768]{0:T(1024)S(1)} %get-tuple-element.21) | copy-start | bytes 9220
  32.1 49.1 %copy-start.51 = (f32[192]{0:T(256)S(1)}, f32[192]{0:T(256)}, u32[]{:S(2)}) copy-start(f32[192]{0:T(256)} %param.23) | copy-start | bytes 2308
  32.1 49.4 %copy-start.50 = (f32[2,192]{1,0:T(2,128)S(1)}, f32[2,192]{1,0:T(2,128)}, u32[]{:S(2)}) copy-start(f32[2,192]{1,0:T(2,128)} %param.21) | copy-start | bytes 4612
  80.6 3.9 collective-permute-start
  80.7 169.5 %all-gather.8.cloned.1.call-start = ((), (), s32[]{:S(2)}) async-start(), calls=%async_computation.13 | async-start | bytes 5898240 | tf_op jit(solution)/shard_map/all_gather | solution.py:113
  81.6 59.8 %copy-start.41 = (s32[2432]{0:T(1024)}, s32[2432]{0:T(1024)S(1)}, u32[]{:S(2)}) copy-start(s32[2432]{0:T(1024)S(1)} %fusion.120) | copy-start | bytes 29188
  89.7 51.7 %copy-start.39 = (s32[2304]{0:T(1024)}, s32[2304]{0:T(1024)S(1)}, u32[]{:S(2)}) copy-start(s32[2304]{0:T(1024)S(1)} %eq.201) | copy-start | bytes 27652
  149.8 3.9 collective-permute-start.1
  157.1 42.0 %collective-permute-start.2 = (bf16[576,768]{1,0:T(8,128)(2,1)S(1)}, bf16[576,768]{1,0:T(8,128)(2,1)S(1)}, u32[]{:S(2)}, u32[]{:S(2)}) collective-permute-start(bf16[576,768]{1,0:T(8,128)(2,1)S(1)} %slice.292), channel_id=1, source_target_pairs={{0,2},{1,3},{2,0},{3,1},{4,6},{5,7},{6,4},{7,5},{8,10},{9,11},{10,... | collective-permute-start | bytes 2654216 | tf_op jit(solution)/shard_map/ppermute | solution.py:175
  158.5 15.1 %copy-start.46 = (f32[768]{0:T(1024)S(1)}, f32[768]{0:T(1024)}, u32[]{:S(2)}) copy-start(f32[768]{0:T(1024)} %param.26) | copy-start | bytes 9220
  158.5 15.2 %copy-start.35 = (f32[768]{0:T(1024)S(1)}, f32[768]{0:T(1024)}, u32[]{:S(2)}) copy-start(f32[768]{0:T(1024)} %param.18) | copy-start | bytes 9220
  173.6 25.4 %copy-start.44 = (f32[2,768]{1,0:T(2,128)S(1)}, f32[2,768]{1,0:T(2,128)}, u32[]{:S(2)}) copy-start(f32[2,768]{1,0:T(2,128)} %param.24) | copy-start | bytes 18436
  178.8 21.4 %copy-start.25 = (f32[1200]{0:T(1024)}, f32[1200]{0:T(1024)S(1)}, u32[]{:S(2)}) copy-start(f32[1200]{0:T(1024)S(1)} %convolution_reduce_fusion) | copy-start | bytes 14404
  199.0 31.7 %copy-start.45 = (f32[768]{0:T(1024)}, f32[768]{0:T(1024)S(1)}, u32[]{:S(2)}) copy-start(f32[768]{0:T(1024)S(1)} %get-tuple-element.24) | copy-start | bytes 9220
  199.1 78.9 %copy-start.34 = (f32[768]{0:T(1024)}, f32[768]{0:T(1024)S(1)}, u32[]{:S(2)}) copy-start(f32[768]{0:T(1024)S(1)} %get-tuple-element.23) | copy-start | bytes 9220
  200.2 26.5 %all-to-all-start.1 = ((bf16[8,72,768]{2,1,0:T(8,128)(2,1)}), bf16[8,72,768]{2,1,0:T(8,128)(2,1)S(1)}, u32[]{:S(2)}, u32[]{:S(2)}) async-start(bf16[8,72,768]{2,1,0:T(8,128)(2,1)} %bitcast.21), calls=%async_computation.1 | async-start | bytes 1769472 | tf_op jit(solution)/shard_map/all_to_all | solution.py:179
  203.7 335.6 %reduce-scatter.5.cloned.1.call-start = ((), (), s32[]{:S(2)}) async-start(), calls=%async_computation.11 | async-start | bytes 5898240 | tf_op jit(solution)/shard_map/reduce_scatter | solution.py:226
  230.8 47.2 %copy-start.31 = (f32[1200]{0:T(1024)}, f32[1200]{0:T(1024)S(1)}, u32[]{:S(2)}) copy-start(f32[1200]{0:T(1024)S(1)} %add_rsqrt_fusion) | copy-start | bytes 14404
  231.2 10.5 %copy-start.16 = (bf16[1200,768]{1,0:T(8,128)(2,1)S(1)}, bf16[1200,768]{1,0:T(8,128)(2,1)}, u32[]{:S(2)}) copy-start(bf16[1200,768]{1,0:T(8,128)(2,1)} %fusion.65) | copy-start | bytes 5529604
  250.1 289.3 %reduce-scatter.3.cloned.1.call-start = ((), (), s32[]{:S(2)}) async-start(), calls=%async_computation.10 | async-start | bytes 5898240 | tf_op jit(solution)/shard_map/reduce_scatter | solution.py:225
  250.2 14.4 %copy-start.3 = (f32[1200,768]{1,0:T(8,128)S(1)}, f32[1200,768]{1,0:T(8,128)}, u32[]{:S(2)}) copy-start(f32[1200,768]{1,0:T(8,128)} %copy-done.1) | copy-start | bytes 11059204
  264.5 13.4 %copy-start.52 = (bf16[1200,3072]{1,0:T(8,128)(2,1)}, bf16[1200,3072]{1,0:T(8,128)(2,1)S(1)}, u32[]{:S(2)}) copy-start(bf16[1200,3072]{1,0:T(8,128)(2,1)S(1)} %get-tuple-element.73) | copy-start | bytes 22118404
  264.6 13.5 %copy-start.17 = (bf16[1200,768]{1,0:T(8,128)(2,1)S(1)}, bf16[1200,768]{1,0:T(8,128)(2,1)}, u32[]{:S(2)}) copy-start(bf16[1200,768]{1,0:T(8,128)(2,1)} %fusion.65) | copy-start | bytes 5529604
  312.0 38.1 %copy-start.13 = (bf16[8,72,768]{2,1,0:T(8,128)(2,1)}, bf16[8,72,768]{2,1,0:T(8,128)(2,1)S(1)}, u32[]{:S(2)}) copy-start(bf16[8,72,768]{2,1,0:T(8,128)(2,1)S(1)} %all_to_all.41) | copy-start | bytes 2654212
  312.0 23.2 %collective-permute-start.3 = (bf16[576,768]{1,0:T(8,128)(2,1)S(1)}, bf16[576,768]{1,0:T(8,128)(2,1)S(1)}, u32[]{:S(2)}, u32[]{:S(2)}) collective-permute-start(bf16[576,768]{1,0:T(8,128)(2,1)S(1)} %bitcast.212), channel_id=1, source_target_pairs={{0,2},{1,3},{2,0},{3,1},{4,6},{5,7},{6,4},{7,5},{8,10},{9,11},{10,... | collective-permute-start | bytes 2654216 | tf_op jit(solution)/shard_map/ppermute | solution.py:230
  335.2 14.9 %copy-start.21 = (bf16[576,768]{1,0:T(8,128)(2,1)}, bf16[576,768]{1,0:T(8,128)(2,1)S(1)}, u32[]{:S(2)}) copy-start(bf16[576,768]{1,0:T(8,128)(2,1)S(1)} %collective-permute-done.3) | copy-start | bytes 2654212
  336.6 13.4 %collective-permute-start.4 = (bf16[1152,768]{1,0:T(8,128)(2,1)}, bf16[1152,768]{1,0:T(8,128)(2,1)}, u32[]{:S(2)}, u32[]{:S(2)}) collective-permute-start(bf16[1152,768]{1,0:T(8,128)(2,1)} %pad_maximum_fusion.2), channel_id=1, source_target_pairs={{0,1},{1,0},{2,3},{3,2},{4,5},{5,4},{6,7},{7,6},{8,9},{9,8},{10,11... | collective-permute-start | bytes 5308424 | tf_op jit(solution)/shard_map/ppermute | solution.py:231
  360.4 15.3 %slice-start = ((s8[11206656]{0:T(1024)(128)(4,1)}), s8[4194304]{0:T(1024)(128)(4,1)S(1)}, s32[]{:S(2)}) async-start(s8[11206656]{0:T(1024)(128)(4,1)} %bitcast.203), calls=%async_computation.15 | async-start | bytes 8388608
  360.4 15.3 %slice-start.1 = ((s8[11206656]{0:T(1024)(128)(4,1)}), s8[4194304]{0:T(1024)(128)(4,1)S(1)}, s32[]{:S(2)}) async-start(s8[11206656]{0:T(1024)(128)(4,1)} %bitcast.203), calls=%async_computation.16 | async-start | bytes 8388608
  366.8 8.9 %slice-start.2 = ((s8[11206656]{0:T(1024)(128)(4,1)}), s8[2818048]{0:T(1024)(128)(4,1)S(1)}, s32[]{:S(2)}) async-start(s8[11206656]{0:T(1024)(128)(4,1)} %bitcast.203), calls=%async_computation.17 | async-start | bytes 5636096
  396.9 20.9 %copy-start.49 = (f32[768]{0:T(1024)S(1)}, f32[768]{0:T(1024)}, u32[]{:S(2)}) copy-start(f32[768]{0:T(1024)} %all-reduce.4) | copy-start | bytes 9220
  417.3 58.1 %collective-permute-start.5 = (bf16[1152,768]{1,0:T(8,128)(2,1)}, bf16[1152,768]{1,0:T(8,128)(2,1)}, u32[]{:S(2)}, u32[]{:S(2)}) collective-permute-start(bf16[1152,768]{1,0:T(8,128)(2,1)} %slice.288), channel_id=1, source_target_pairs={{0,1},{1,0},{2,3},{3,2},{4,5},{5,4},{6,7},{7,6},{8,9},{9,8},{10,11... | collective-permute-start | bytes 5308424 | tf_op jit(solution)/shard_map/ppermute | solution.py:173
  431.0 17.2 %all-to-all-start.2 = ((bf16[4,576,192]{1,2,0:T(8,128)(2,1)}), bf16[4,576,192]{1,2,0:T(8,128)(2,1)S(1)}, u32[]{:S(2)}, u32[]{:S(2)}) async-start(bf16[4,576,192]{1,2,0:T(8,128)(2,1)} %bitcast.29), calls=%async_computation.2 | async-start | bytes 1966080 | tf_op jit(solution)/shard_map/all_to_all | solution.py:262
  436.2 19.8 %copy-start.43 = (f32[3072]{0:T(1024)S(1)}, f32[3072]{0:T(1024)}, u32[]{:S(2)}) copy-start(f32[3072]{0:T(1024)} %get-tuple-element.72) | copy-start | bytes 36868
  436.2 19.8 %copy-start.48 = (f32[768]{0:T(1024)S(1)}, f32[768]{0:T(1024)}, u32[]{:S(2)}) copy-start(f32[768]{0:T(1024)} %get-tuple-element.13) | copy-start | bytes 9220
  436.2 19.8 %copy-start.47 = (f32[768]{0:T(1024)S(1)}, f32[768]{0:T(1024)}, u32[]{:S(2)}) copy-start(f32[768]{0:T(1024)} %get-tuple-element.18) | copy-start | bytes 9220
  436.2 19.8 %copy-start.38 = (f32[768]{0:T(1024)S(1)}, f32[768]{0:T(1024)}, u32[]{:S(2)}) copy-start(f32[768]{0:T(1024)} %get-tuple-element.40) | copy-start | bytes 9220
  436.2 19.8 %copy-start.26 = (f32[1200]{0:T(1024)S(1)}, f32[1200]{0:T(1024)}, u32[]{:S(2)}) copy-start(f32[1200]{0:T(1024)} %copy-done.25) | copy-start | bytes 14404
  436.2 19.8 %copy-start.30 = (f32[1200]{0:T(1024)S(1)}, f32[1200]{0:T(1024)}, u32[]{:S(2)}) copy-start(f32[1200]{0:T(1024)} %get-tuple-element.33) | copy-start | bytes 14404
  448.2 18.1 %all-to-all-start.3 = ((bf16[4,624,192]{1,2,0:T(8,128)(2,1)}), bf16[4,624,192]{1,2,0:T(8,128)(2,1)}, u32[]{:S(2)}, u32[]{:S(2)}) async-start(bf16[4,624,192]{1,2,0:T(8,128)(2,1)} %bitcast.31), calls=%async_computation.3 | async-start | bytes 1966080 | tf_op jit(solution)/shard_map/all_to_all | solution.py:262
  466.3 39.6 %all-to-all-start.7 = ((bf16[4,624,192]{1,2,0:T(8,128)(2,1)}), bf16[4,624,192]{1,2,0:T(8,128)(2,1)S(1)}, u32[]{:S(2)}, u32[]{:S(2)}) async-start(bf16[4,624,192]{1,2,0:T(8,128)(2,1)} %bitcast.211), calls=%async_computation.7 | async-start | bytes 1966080 | tf_op jit(solution)/shard_map/all_to_all | solution.py:262
  481.1 22.2 %collective-permute-start.6 = (bf16[576,768]{1,0:T(8,128)(2,1)}, bf16[576,768]{1,0:T(8,128)(2,1)S(1)}, u32[]{:S(2)}, u32[]{:S(2)}) collective-permute-start(bf16[576,768]{1,0:T(8,128)(2,1)} %slice.291), channel_id=1, source_target_pairs={{0,2},{1,3},{2,0},{3,1},{4,6},{5,7},{6,4},{7,5},{8,10},{9,11},{10,... | collective-permute-start | bytes 2654216 | tf_op jit(solution)/shard_map/ppermute | solution.py:175
  496.5 14.1 %copy-start.32 = (s32[4616]{0:T(1024)S(1)}, s32[4616]{0:T(1024)}, u32[]{:S(2)}) copy-start(s32[4616]{0:T(1024)} %get-tuple-element.45) | copy-start | bytes 55396
  505.9 30.6 %all-to-all-start.5 = ((bf16[8,72,768]{2,1,0:T(8,128)(2,1)}), bf16[8,72,768]{2,1,0:T(8,128)(2,1)S(1)}, u32[]{:S(2)}, u32[]{:S(2)}) async-start(bf16[8,72,768]{2,1,0:T(8,128)(2,1)} %bitcast.216), calls=%async_computation.5 | async-start | bytes 1769472 | tf_op jit(solution)/shard_map/all_to_all | solution.py:179
  510.6 171.6 %all-reduce.8.cloned.1.call-start = ((), (), s32[]{:S(2)}) async-start(), calls=%async_computation.14 | async-start | bytes 7077888 | tf_op jit(solution)/shard_map/psum | solution.py:250
  543.3 81.4 %all-to-all-start.6 = ((bf16[4,576,192]{1,2,0:T(8,128)(2,1)}), bf16[4,576,192]{1,2,0:T(8,128)(2,1)S(1)}, u32[]{:S(2)}, u32[]{:S(2)}) async-start(bf16[4,576,192]{1,2,0:T(8,128)(2,1)} %bitcast.43), calls=%async_computation.6 | async-start | bytes 1966080 | tf_op jit(solution)/shard_map/all_to_all | solution.py:262
  (30 other events, 139.2 us)
Sparse Core Ops, SparseCore 0:
  80.8 36.5 all-gather.5
  150.1 55.4 all-gather.7
  250.2 47.7 reduce-scatter.4
  350.1 46.8 reduce-scatter.2
  539.5 142.6 all-reduce.7
where the time goes:
time: 705 us; the launch traced here: 697 us
  matrix products  260 us (37%)
  blocking collectives  175 us (25%)
  local copies, waits for them, and re-layouts  80 us (11%)
  waiting for transfers between devices  72.2 us (10%)
  other arithmetic  63.8 us (9%)
  starting transfers between devices  29.5 us (4%)
  between operations  16.1 us (2%)
    dot_general x14, matrix products, mul(): lax.dot_general(left, right, (((1,), (0,)), ((), ())), preferred_element_...  149 us
    all_to_all x1, blocking collectives, body(): lax.all_to_all(send_rows.reshape(peers, 2, block, width), 'tok', split_ax...  48.4 us
    dot_general x3, matrix products, mul_t1(): lax.dot_general(left, right, (((1,), (1,)), ((), ())), preferred_element_...  44.5 us
    psum x1, waiting for transfers between devices, body(): d_qkv_total = lax.psum(d_qkv_weight.astype(BF), 'tok').astype(F32)  42.5 us
    psum x1, blocking collectives, body(): small = lax.psum(jnp.concatenate([small, first_pair]), ('tok', 'tp'))  38.3 us
    dot_general x5, matrix products, mul_t0(): lax.dot_general(left, right, (((0,), (0,)), ((), ())), preferred_element_...  30.6 us
    all_to_all x1, blocking collectives, across(): lax.all_to_all(rows.reshape(peers, block, width), 'tok', split_axis=0, co...  27.2 us
    psum x1, blocking collectives, body(): d_qv_bias = lax.psum(d_qv_bias, 'tok')  23.7 us
  transfers between devices with their start and end apart: 18, of which 7 were waited for; matrix products, arithmetic and copies ran while one was open for 52% of the time, Pallas kernels for 0%

commit v1 on v0

--- a/solution.py
+++ b/solution.py
@@ -274,7 +274,7 @@
     small = lax.psum(jnp.concatenate([small, first_pair]), ("tok", "tp"))
     small_cols = columns_of(small[shares:], part, shares)
     d_up_bias = lax.dynamic_slice_in_dim(small, part, 1, 0).reshape(width)
-    d_qv_bias = lax.psum(d_qv_bias, "tok")
+    d_qv_bias = jnp.sum(lax.all_gather(d_qv_bias, axis_name="tok"), 0)
     return (
         layer_out,
         d_tokens,

time: 705 us -> 705 us (level)
    all_gather x0 -> x1, blocking collectives: none -> 28.6 us  [body(): d_qv_bias = jnp.sum(lax.all_gather(d_qv_bias, axis_name='tok'), 0)]
    psum x1 -> x0, blocking collectives: 23.7 us -> none  [body(): d_qv_bias = lax.psum(d_qv_bias, 'tok')]
where the time goes in v1:
time: 705 us; the launch traced here: 697 us
  matrix products  260 us (37%)
  blocking collectives  182 us (26%)
  local copies, waits for them, and re-layouts  80 us (11%)
  waiting for transfers between devices  66.1 us (9%)
  other arithmetic  64.4 us (9%)
  starting transfers between devices  29.5 us (4%)
  between operations  16.1 us (2%)
    dot_general x14, matrix products, mul(): lax.dot_general(left, right, (((1,), (0,)), ((), ())), preferred_element_...  149 us
    all_to_all x1, blocking collectives, body(): lax.all_to_all(send_rows.reshape(peers, 2, block, width), 'tok', split_ax...  48.4 us
    dot_general x3, matrix products, mul_t1(): lax.dot_general(left, right, (((1,), (1,)), ((), ())), preferred_element_...  44.4 us
    psum x1, blocking collectives, body(): small = lax.psum(jnp.concatenate([small, first_pair]), ('tok', 'tp'))  39.4 us
    psum x1, waiting for transfers between devices, body(): d_qkv_total = lax.psum(d_qkv_weight.astype(BF), 'tok').astype(F32)  36.4 us
    dot_general x5, matrix products, mul_t0(): lax.dot_general(left, right, (((0,), (0,)), ((), ())), preferred_element_...  30.6 us
    all_gather x1, blocking collectives, body(): d_qv_bias = jnp.sum(lax.all_gather(d_qv_bias, axis_name='tok'), 0)  28.6 us
    all_to_all x1, blocking collectives, across(): lax.all_to_all(rows.reshape(peers, block, width), 'tok', split_axis=0, co...  27.2 us
  transfers between devices with their start and end apart: 18, of which 7 were waited for; matrix products, arithmetic and copies ran while one was open for 52% of the time, Pallas kernels for 0%

profile of v1, /device:TPU:0, one launch (start us, length us, event | category | flops | bytes accessed | tf_op | source)
XLA Modules:
  0.0 697.2 jit_solution(2372863380445407270)
XLA Ops:
  16.0 14.7 %fusion.135 = (f32[1152]{0:T(1024)S(1)}, f32[1152,768]{1,0:T(8,128)S(1)}) fusion(bf16[4616,768]{1,0:T(8,128)(2,1)} %param.15, s32[4616]{0:T(1024)S(1)} %get-tuple-element.46), kind=kOutput, calls=%fused_computation.269 | convolution fusion | flops 8174084096 | bytes 10652192 | tf_op jit(solution)/shard_map/dot_general | solution.py:37
  32.1 48.4 %all_to_all.40 = bf16[8,2,72,768]{3,2,1,0:T(8,128)(2,1)S(1)} all-to-all(bf16[8,2,72,768]{3,2,1,0:T(8,128)(2,1)S(1)} %broadcast_select_fusion), channel_id=1, replica_groups=mesh['tok'=8,'tp'=4] {'tok'}, dimensions={0} | all-to-all | bytes 3538944 | tf_op jit(solution)/shard_map/all_to_all | solution.py:130
  85.6 3.9 pad_maximum_fusion
  89.7 12.9 %fusion.44 = bf16[2432,768]{1,0:T(8,128)(2,1)} fusion(bf16[2304,768]{1,0:T(8,128)(2,1)} %bitcast.219, s32[2304]{0:T(1024)S(1)} %eq.201, s32[2432]{0:T(1024)S(1)} %fusion.120), kind=kOutput, calls=%fused_computation.64 | convolution fusion | flops 8614182912 | bytes 7293440 | tf_op jit(solution)/shard_map/dot_general | solution.py:37
  102.6 3.8 select_reduce_fusion
  106.5 6.2 add_convert_fusion
  112.7 7.5 %reshape.344 = bf16[8,304,3,3,64]{1,0,4,3,2:T(8,128)(2,1)} reshape(bf16[2432,576]{0,1:T(8,128)(2,1)} %add_convert_fusion) | data formatting | bytes 5603328 | tf_op jit(solution)/shard_map/reshape | solution.py:155
  125.7 8.3 %fusion.136 = (f32[8,3,304]{2,1,0:T(4,128)S(1)}, f32[8,3,304,304]{2,3,1,0:T(8,128)}) fusion(pred[8,304,304]{1,2,0:T(8,128)(4,1)} %compare_and_fusion, bf16[8,304,1,3,64]{1,0,4,3,2:T(8,128)(2,1)S(1)} %get-tuple-element.38, bf16[8,304,1,3,64]{1,0,4,3,2:T(8,128)(2,1)S(1)} %get-tuple-element.37), kind=kOutput, calls=%fused_computation.270 | convolution fusion | flops 292774176 | bytes 11508224 | tf_op jit(solution)/shard_map/sub | solution.py:161
  134.0 5.8 fusion.83
  141.4 4.1 fusion.53
  150.0 3.7 collective-permute-done.1
  158.5 15.1 %fusion.16 = f32[1200,768]{1,0:T(8,128)S(1)} fusion(bf16[4616,768]{1,0:T(8,128)(2,1)} %param.15, s32[4616]{0:T(1024)S(1)} %get-tuple-element.47), kind=kOutput, calls=%fused_computation.20 | convolution fusion | flops 8513750528 | bytes 10795040 | tf_op jit(solution)/shard_map/dot_general | solution.py:37
  178.8 20.2 %all-gather.3 = f32[4,1,768]{2,1,0:T(1,128)S(1)} all-gather(f32[1,1,768]{2,1,0:T(1,128)S(1)} %reshape.376), channel_id=1, replica_groups=mesh['tok'=8,'tp'=4] {'tp'}, dimensions={0}, use_global_device_ids=true | all-gather | bytes 15360 | tf_op jit(solution)/shard_map/all_gather | solution.py:195
  200.2 3.6 all-to-all-start.1
  203.8 14.8 %fusion.65 = bf16[1200,768]{1,0:T(8,128)(2,1)} fusion(bf16[4616,768]{1,0:T(8,128)(2,1)} %param.29, s32[4616]{0:T(1024)S(1)} %get-tuple-element.47), kind=kOutput, calls=%fused_computation.100 | convolution fusion | flops 8514672128 | bytes 8951840 | tf_op jit(solution)/shard_map/dot_general | solution.py:37
  218.6 6.6 copy.121
  231.2 10.5 %multiply_convert_fusion = (bf16[1200,3072]{1,0:T(8,128)(2,1)S(1)}, f32[1200,3072]{1,0:T(8,128)}) fusion(f32[3072]{0:T(1024)S(1)} %bitcast.230, bf16[768,3072]{0,1:T(8,128)(2,1)S(1)} %bitcast.211, f32[768]{0:T(1024)S(1)} %get-tuple-element.24, f32[768]{0:T(1024)S(1)} %get-tuple-element.23, f32[1200]{0:T(1024)S(1)} %add_rsqrt_fusion, ...), kind=kOutput, calls=%fused_computation.34 | convolution fusion | flops 5691801600 | bytes 31440960 | tf_op jit(solution)/shard_map/dot_general | solution.py:37
  241.7 8.3 %convolution_convert_fusion = bf16[3072,768]{1,0:T(8,128)(2,1)} fusion(bf16[1200,3072]{1,0:T(8,128)(2,1)S(1)} %get-tuple-element.67, bf16[1200,768]{1,0:T(8,128)(2,1)S(1)} %copy-done.16), kind=kOutput, calls=%fused_computation.65 | convolution fusion | flops 5664669696 | bytes 13934592 | tf_op jit(solution)/shard_map/dot_general | solution.py:41
  250.2 14.4 %convert_reduce_fusion = (f32[3072]{0:T(1024)}, bf16[1200,3072]{1,0:T(8,128)(2,1)S(1)}) fusion(f32[1200,3072]{1,0:T(8,128)} %get-tuple-element.68, bf16[1200,768]{1,0:T(8,128)(2,1)} %fusion.65, bf16[3072,768]{1,0:T(8,128)(2,1)} %all-gather.10.cloned.1.call-done), kind=kOutput, calls=%fused_computation.33 | convolution fusion | flops 5706544128 | bytes 28692480 | tf_op jit(solution)/shard_map/dot_general | solution.py:45
  264.6 13.4 %multiply_reduce_fusion.2 = (f32[768]{0:T(1024)}, f32[1200]{0:T(1024)S(1)}, f32[1200]{0:T(1024)S(1)}, f32[768]{0:T(1024)}, f32[1200,768]{1,0:T(8,128)S(1)}) fusion(f32[1200]{0:T(1024)S(1)} %add_rsqrt_fusion, f32[1200]{0:T(1024)S(1)} %broadcast_multiply_fusion.2, f32[1200,768]{1,0:T(8,128)S(1)} %copy-done.3, bf16[576,768]{1,0:T(8,128)(2,1)S(1)} %bitcast.201, ...), kind=kOutput, calls=%fused_computation.86 | convolution fusion | flops 5673365504 | bytes 20382144 | tf_op jit(solution)/shard_map/dot_general | solution.py:45
  278.0 4.2 fusion.60
  284.8 27.2 %all_to_all.41 = bf16[8,72,768]{2,1,0:T(8,128)(2,1)S(1)} all-to-all(bf16[8,72,768]{2,1,0:T(8,128)(2,1)S(1)} %bitcast.220), channel_id=1, replica_groups=mesh['tok'=8,'tp'=4] {'tok'}, dimensions={0} | all-to-all | bytes 1769472 | tf_op jit(solution)/shard_map/all_to_all | solution.py:179
  317.4 17.8 %all-reduce.4 = f32[768]{0:T(1024)} all-reduce(f32[768]{0:T(1024)} %dynamic-update-slice), channel_id=1, replica_groups=mesh['tok'=8,'tp'=4] {'tp'}, use_global_device_ids=true, to_apply=%add.4 | all-reduce | flops 768 | bytes 6144
  336.6 10.9 %convolution_convert_fusion.1 = bf16[768,3072]{1,0:T(8,128)(2,1)S(1)} fusion(bf16[1200,3072]{1,0:T(8,128)(2,1)} %copy-done.52, f32[768]{0:T(1024)} %copy-done.45, f32[768]{0:T(1024)} %copy-done.34, f32[1200]{0:T(1024)} %copy-done.31, f32[1200]{0:T(1024)S(1)} %broadcast_multiply_fusion.2, f32[1200,768]{1,0:T(8,128)} %copy-done.1, ...), kind=kOutput, calls=%fused_computation.66 | convolution fusion | flops 5672042496 | bytes 16683072 | tf_op jit(solution)/shard_map/dot_general | solution.py:41
  350.0 7.7 %fusion.56 = bf16[2432,192]{0,1:T(8,128)(2,1)} fusion(s32[2304]{0:T(1024)} %copy-done.39, s32[2432]{0:T(1024)} %copy-done.41, bf16[192,768]{1,0:T(8,128)(2,1)} %param.22, bf16[1152,768]{1,0:T(8,128)(2,1)} %collective-permute-done.4, bf16[576,768]{1,0:T(8,128)(2,1)S(1)} %collective-permute-done.3, bf16[576,768]{1,0:T(8,128)(2,1)S(1)} %bitcast.216), kind=kOutput, calls=%fused_computation.81 | convolution fusion | flops 2848284672 | bytes 4786688 | tf_op jit(solution)/shard_map/dot_general | solution.py:37
  360.4 6.4 fusion.75
  366.8 8.9 %multiply_reduce_fusion = (f32[8,3,304]{2,1,0:T(4,128)S(1)}, f32[8,3,304,304]{2,3,1,0:T(8,128)}) fusion(f32[8,3,304,304]{2,3,1,0:T(8,128)} %get-tuple-element.66, f32[8,3,304]{2,1,0:T(4,128)S(1)} %copy-done.29, bf16[8,304,1,3,64]{1,0,4,3,2:T(8,128)(2,1)S(1)} %copy-done.18, bf16[8,304,3,64]{1,0,3,2:T(8,128)(2,1)S(1)} %reshape.354), kind=kOutput, calls=%fused_computation.40 | convolution fusion | flops 290548608 | bytes 19670016 | tf_op jit(solution)/shard_map/rqhe,rkhe->rhqk/dot_general | solution.py:235
  375.7 6.1 multiply_convert_fusion.1
  386.0 4.1 copy.131
  390.1 6.7 convert_element_type.200
  396.9 16.6 %fusion.62 = f32[2304,768]{1,0:T(8,128)} fusion(bf16[768,576]{0,1:T(8,128)(2,1)S(1)} %bitcast.194, bf16[2432,576]{0,1:T(8,128)(2,1)} %convert_element_type.200, s32[2304]{0:T(1024)S(1)} %copy-done.40, s32[2432]{0:T(1024)S(1)} %copy-done.42), kind=kOutput, calls=%fused_computation.98 | convolution fusion | flops 8500396032 | bytes 10783232 | tf_op jit(solution)/shard_map/dot_general | solution.py:45
  413.5 3.8 slice.288
  417.7 10.6 %fusion.64 = bf16[1200,768]{1,0:T(8,128)(2,1)S(1)} fusion(bf16[1200,3072]{1,0:T(8,128)(2,1)} %copy-done.54, bf16[3072,768]{1,0:T(8,128)(2,1)} %all-gather.10.cloned.1.call-done, f32[768]{0:T(1024)S(1)} %copy-done.49, f32[1200,768]{1,0:T(8,128)} %copy-done.1, bf16[576,768]{1,0:T(8,128)(2,1)S(1)} %bitcast.204, f32[1200]{0:T(1024)S(1)} %fusion.123), kind=kOutput, calls=%fused_computation.99 | convolution fusion | flops 5667840000 | bytes 18513600 | tf_op jit(solution)/shard_map/dot_general | solution.py:37
  437.5 10.7 %all-to-all-done.2 = bf16[4,576,192]{1,2,0:T(8,128)(2,1)S(1)} async-done(((bf16[4,576,192]{1,2,0:T(8,128)(2,1)}), bf16[4,576,192]{1,2,0:T(8,128)(2,1)S(1)}, u32[]{:S(2)}, u32[]{:S(2)}) %all-to-all-start.2) | async-done | bytes 884768 | tf_op jit(solution)/shard_map/all_to_all | solution.py:262
  448.2 4.2 all-to-all-start.3
  462.2 4.1 all-to-all-done.3
  466.3 3.5 all-to-all-start.7
  483.0 13.4 %fusion.2 = f32[4616,192]{0,1:T(8,128)} fusion(bf16[2496,192]{0,1:T(8,128)(2,1)} %reshape.351, s32[4616]{0:T(1024)S(1)} %copy-done.33), kind=kOutput, calls=%fused_computation.3 | convolution fusion | flops 4435791360 | bytes 4522016 | tf_op jit(solution)/shard_map/dot_general | solution.py:37
  496.5 6.8 collective-permute-done.6
  505.9 4.7 all-to-all-start.5
  510.7 13.9 %fusion.40 = bf16[4616,192]{0,1:T(8,128)(2,1)} fusion(f32[4616,192]{0,1:T(8,128)} %fusion.2, bf16[2304,192]{0,1:T(8,128)(2,1)} %reshape.349, s32[4616]{0:T(1024)S(1)} %copy-done.32), kind=kOutput, calls=%fused_computation.57 | convolution fusion | flops 4096349184 | bytes 6220832 | tf_op jit(solution)/shard_map/dot_general | solution.py:37
  529.0 4.0 fusion.86
  543.3 3.7 all-to-all-start.6
  547.1 13.5 %fusion.1 = f32[4616,192]{0,1:T(8,128)} fusion(bf16[2496,192]{0,1:T(8,128)(2,1)} %reshape.359, s32[4616]{0:T(1024)S(1)} %copy-done.33), kind=kOutput, calls=%fused_computation.2 | convolution fusion | flops 4435791360 | bytes 4522016 | tf_op jit(solution)/shard_map/dot_general | solution.py:37
  560.7 28.6 %all-gather.4 = f32[8,2,192]{2,1,0:T(2,128)S(1)} all-gather(f32[1,2,192]{2,1,0:T(2,128)S(1)} %maximum_bitcast_fusion), channel_id=4, replica_groups=mesh['tok'=8,'tp'=4] {'tok'}, dimensions={0}, use_global_device_ids=true | all-gather | bytes 13824 | tf_op jit(solution)/shard_map/all_gather | solution.py:277
  589.9 39.4 %psum.37 = f32[11,768]{1,0:T(8,128)S(1)} all-reduce(f32[11,768]{1,0:T(8,128)S(1)} %concatenate.16), channel_id=1, replica_groups=mesh['tok'=8,'tp'=4] {'tok','tp'}, use_global_device_ids=true, to_apply=%region_32.33 | all-reduce | flops 8448 | bytes 67584 | tf_op jit(solution)/shard_map/psum | solution.py:274
  632.8 13.6 %fusion.39 = f32[4616,192]{0,1:T(8,128)} fusion(f32[4616,192]{0,1:T(8,128)} %fusion.1, bf16[2304,192]{0,1:T(8,128)(2,1)S(1)} %reshape.357, s32[4616]{0:T(1024)S(1)} %copy-done.32), kind=kOutput, calls=%fused_computation.56 | convolution fusion | flops 4095462912 | bytes 7993376 | tf_op jit(solution)/shard_map/dot_general | solution.py:37
  646.3 36.4 %all-reduce.8.cloned.1.call-done = (bf16[768,3,192]{0,2,1:T(8,128)(2,1)}, bf16[192,768]{1,0:T(8,128)(2,1)}, bf16[768,768]{1,0:T(8,128)(2,1)}, bf16[768,768]{1,0:T(8,128)(2,1)}) async-done(((bf16[768,3,192]{0,2,1:T(8,128)(2,1)}, bf16[192,768]{1,0:T(8,128)(2,1)}, bf16[768,768]{1,0:T(8,128)(2,1)}, bf16[768,768]{1,0:T(8,128)(2,1)}), (bf16[768,3,192]{0,2,1:T(8,128)(2,1)}, bf16[192,768]{1,0:T(8,128)(2,1)}, ...) | async-done | bytes 3538960 | tf_op jit(solution)/shard_map/psum | solution.py:250
  (286 shorter events, 123.7 us)
Async XLA Ops:
  7.2 99.3 %copy-start = (bf16[768,3,192]{0,2,1:T(8,128)(2,1)S(1)}, bf16[768,3,192]{0,2,1:T(8,128)(2,1)}, u32[]{:S(2)}) copy-start(bf16[768,3,192]{0,2,1:T(8,128)(2,1)} %param.20) | copy-start | bytes 2654212
  7.2 211.4 %all-gather.8.cloned.1.call-start = ((), (), s32[]{:S(2)}) async-start(), calls=%async_computation.12 | async-start | bytes 5898240 | tf_op jit(solution)/shard_map/all_gather | solution.py:112
  8.1 23.2 %copy-start.23 = (f32[768]{0:T(1024)}, f32[768]{0:T(1024)S(1)}, u32[]{:S(2)}) copy-start(f32[768]{0:T(1024)S(1)} %get-tuple-element.21) | copy-start | bytes 9220
  32.1 49.1 %copy-start.51 = (f32[192]{0:T(256)S(1)}, f32[192]{0:T(256)}, u32[]{:S(2)}) copy-start(f32[192]{0:T(256)} %param.23) | copy-start | bytes 2308
  32.1 49.4 %copy-start.50 = (f32[2,192]{1,0:T(2,128)S(1)}, f32[2,192]{1,0:T(2,128)}, u32[]{:S(2)}) copy-start(f32[2,192]{1,0:T(2,128)} %param.21) | copy-start | bytes 4612
  80.6 3.9 collective-permute-start
  80.7 169.5 %all-gather.10.cloned.1.call-start = ((), (), s32[]{:S(2)}) async-start(), calls=%async_computation.13 | async-start | bytes 5898240 | tf_op jit(solution)/shard_map/all_gather | solution.py:113
  81.6 59.8 %copy-start.41 = (s32[2432]{0:T(1024)}, s32[2432]{0:T(1024)S(1)}, u32[]{:S(2)}) copy-start(s32[2432]{0:T(1024)S(1)} %fusion.120) | copy-start | bytes 29188
  89.7 51.8 %copy-start.39 = (s32[2304]{0:T(1024)}, s32[2304]{0:T(1024)S(1)}, u32[]{:S(2)}) copy-start(s32[2304]{0:T(1024)S(1)} %eq.201) | copy-start | bytes 27652
  149.8 3.9 collective-permute-start.1
  157.1 42.0 %collective-permute-start.2 = (bf16[576,768]{1,0:T(8,128)(2,1)S(1)}, bf16[576,768]{1,0:T(8,128)(2,1)S(1)}, u32[]{:S(2)}, u32[]{:S(2)}) collective-permute-start(bf16[576,768]{1,0:T(8,128)(2,1)S(1)} %slice.292), channel_id=1, source_target_pairs={{0,2},{1,3},{2,0},{3,1},{4,6},{5,7},{6,4},{7,5},{8,10},{9,11},{10,... | collective-permute-start | bytes 2654216 | tf_op jit(solution)/shard_map/ppermute | solution.py:175
  158.5 15.1 %copy-start.46 = (f32[768]{0:T(1024)S(1)}, f32[768]{0:T(1024)}, u32[]{:S(2)}) copy-start(f32[768]{0:T(1024)} %param.26) | copy-start | bytes 9220
  158.5 15.2 %copy-start.35 = (f32[768]{0:T(1024)S(1)}, f32[768]{0:T(1024)}, u32[]{:S(2)}) copy-start(f32[768]{0:T(1024)} %param.18) | copy-start | bytes 9220
  173.7 25.4 %copy-start.44 = (f32[2,768]{1,0:T(2,128)S(1)}, f32[2,768]{1,0:T(2,128)}, u32[]{:S(2)}) copy-start(f32[2,768]{1,0:T(2,128)} %param.24) | copy-start | bytes 18436
  178.8 21.4 %copy-start.25 = (f32[1200]{0:T(1024)}, f32[1200]{0:T(1024)S(1)}, u32[]{:S(2)}) copy-start(f32[1200]{0:T(1024)S(1)} %convolution_reduce_fusion) | copy-start | bytes 14404
  199.1 31.7 %copy-start.45 = (f32[768]{0:T(1024)}, f32[768]{0:T(1024)S(1)}, u32[]{:S(2)}) copy-start(f32[768]{0:T(1024)S(1)} %get-tuple-element.24) | copy-start | bytes 9220
  199.1 78.9 %copy-start.34 = (f32[768]{0:T(1024)}, f32[768]{0:T(1024)S(1)}, u32[]{:S(2)}) copy-start(f32[768]{0:T(1024)S(1)} %get-tuple-element.23) | copy-start | bytes 9220
  200.2 26.5 %all-to-all-start.1 = ((bf16[8,72,768]{2,1,0:T(8,128)(2,1)}), bf16[8,72,768]{2,1,0:T(8,128)(2,1)S(1)}, u32[]{:S(2)}, u32[]{:S(2)}) async-start(bf16[8,72,768]{2,1,0:T(8,128)(2,1)} %bitcast.21), calls=%async_computation.1 | async-start | bytes 1769472 | tf_op jit(solution)/shard_map/all_to_all | solution.py:179
  203.7 335.7 %reduce-scatter.5.cloned.1.call-start = ((), (), s32[]{:S(2)}) async-start(), calls=%async_computation.11 | async-start | bytes 5898240 | tf_op jit(solution)/shard_map/reduce_scatter | solution.py:226
  230.8 47.2 %copy-start.31 = (f32[1200]{0:T(1024)}, f32[1200]{0:T(1024)S(1)}, u32[]{:S(2)}) copy-start(f32[1200]{0:T(1024)S(1)} %add_rsqrt_fusion) | copy-start | bytes 14404
  231.2 10.5 %copy-start.16 = (bf16[1200,768]{1,0:T(8,128)(2,1)S(1)}, bf16[1200,768]{1,0:T(8,128)(2,1)}, u32[]{:S(2)}) copy-start(bf16[1200,768]{1,0:T(8,128)(2,1)} %fusion.65) | copy-start | bytes 5529604
  250.1 289.3 %reduce-scatter.3.cloned.1.call-start = ((), (), s32[]{:S(2)}) async-start(), calls=%async_computation.10 | async-start | bytes 5898240 | tf_op jit(solution)/shard_map/reduce_scatter | solution.py:225
  250.2 14.4 %copy-start.3 = (f32[1200,768]{1,0:T(8,128)S(1)}, f32[1200,768]{1,0:T(8,128)}, u32[]{:S(2)}) copy-start(f32[1200,768]{1,0:T(8,128)} %copy-done.1) | copy-start | bytes 11059204
  264.6 13.4 %copy-start.52 = (bf16[1200,3072]{1,0:T(8,128)(2,1)}, bf16[1200,3072]{1,0:T(8,128)(2,1)S(1)}, u32[]{:S(2)}) copy-start(bf16[1200,3072]{1,0:T(8,128)(2,1)S(1)} %get-tuple-element.73) | copy-start | bytes 22118404
  264.6 13.5 %copy-start.17 = (bf16[1200,768]{1,0:T(8,128)(2,1)S(1)}, bf16[1200,768]{1,0:T(8,128)(2,1)}, u32[]{:S(2)}) copy-start(bf16[1200,768]{1,0:T(8,128)(2,1)} %fusion.65) | copy-start | bytes 5529604
  312.0 38.0 %copy-start.13 = (bf16[8,72,768]{2,1,0:T(8,128)(2,1)}, bf16[8,72,768]{2,1,0:T(8,128)(2,1)S(1)}, u32[]{:S(2)}) copy-start(bf16[8,72,768]{2,1,0:T(8,128)(2,1)S(1)} %all_to_all.41) | copy-start | bytes 2654212
  312.0 23.2 %collective-permute-start.3 = (bf16[576,768]{1,0:T(8,128)(2,1)S(1)}, bf16[576,768]{1,0:T(8,128)(2,1)S(1)}, u32[]{:S(2)}, u32[]{:S(2)}) collective-permute-start(bf16[576,768]{1,0:T(8,128)(2,1)S(1)} %bitcast.214), channel_id=1, source_target_pairs={{0,2},{1,3},{2,0},{3,1},{4,6},{5,7},{6,4},{7,5},{8,10},{9,11},{10,... | collective-permute-start | bytes 2654216 | tf_op jit(solution)/shard_map/ppermute | solution.py:230
  335.1 14.9 %copy-start.21 = (bf16[576,768]{1,0:T(8,128)(2,1)}, bf16[576,768]{1,0:T(8,128)(2,1)S(1)}, u32[]{:S(2)}) copy-start(bf16[576,768]{1,0:T(8,128)(2,1)S(1)} %collective-permute-done.3) | copy-start | bytes 2654212
  336.6 13.4 %collective-permute-start.4 = (bf16[1152,768]{1,0:T(8,128)(2,1)}, bf16[1152,768]{1,0:T(8,128)(2,1)}, u32[]{:S(2)}, u32[]{:S(2)}) collective-permute-start(bf16[1152,768]{1,0:T(8,128)(2,1)} %pad_maximum_fusion.2), channel_id=1, source_target_pairs={{0,1},{1,0},{2,3},{3,2},{4,5},{5,4},{6,7},{7,6},{8,9},{9,8},{10,11... | collective-permute-start | bytes 5308424 | tf_op jit(solution)/shard_map/ppermute | solution.py:231
  360.4 15.3 %slice-start = ((s8[11206656]{0:T(1024)(128)(4,1)}), s8[4194304]{0:T(1024)(128)(4,1)S(1)}, s32[]{:S(2)}) async-start(s8[11206656]{0:T(1024)(128)(4,1)} %bitcast.205), calls=%async_computation.15 | async-start | bytes 8388608
  360.4 15.3 %slice-start.1 = ((s8[11206656]{0:T(1024)(128)(4,1)}), s8[4194304]{0:T(1024)(128)(4,1)S(1)}, s32[]{:S(2)}) async-start(s8[11206656]{0:T(1024)(128)(4,1)} %bitcast.205), calls=%async_computation.16 | async-start | bytes 8388608
  366.8 8.9 %slice-start.2 = ((s8[11206656]{0:T(1024)(128)(4,1)}), s8[2818048]{0:T(1024)(128)(4,1)S(1)}, s32[]{:S(2)}) async-start(s8[11206656]{0:T(1024)(128)(4,1)} %bitcast.205), calls=%async_computation.17 | async-start | bytes 5636096
  396.9 20.9 %copy-start.49 = (f32[768]{0:T(1024)S(1)}, f32[768]{0:T(1024)}, u32[]{:S(2)}) copy-start(f32[768]{0:T(1024)} %all-reduce.4) | copy-start | bytes 9220
  417.3 58.1 %collective-permute-start.5 = (bf16[1152,768]{1,0:T(8,128)(2,1)}, bf16[1152,768]{1,0:T(8,128)(2,1)}, u32[]{:S(2)}, u32[]{:S(2)}) collective-permute-start(bf16[1152,768]{1,0:T(8,128)(2,1)} %slice.288), channel_id=1, source_target_pairs={{0,1},{1,0},{2,3},{3,2},{4,5},{5,4},{6,7},{7,6},{8,9},{9,8},{10,11... | collective-permute-start | bytes 5308424 | tf_op jit(solution)/shard_map/ppermute | solution.py:173
  431.0 17.2 %all-to-all-start.2 = ((bf16[4,576,192]{1,2,0:T(8,128)(2,1)}), bf16[4,576,192]{1,2,0:T(8,128)(2,1)S(1)}, u32[]{:S(2)}, u32[]{:S(2)}) async-start(bf16[4,576,192]{1,2,0:T(8,128)(2,1)} %bitcast.29), calls=%async_computation.2 | async-start | bytes 1966080 | tf_op jit(solution)/shard_map/all_to_all | solution.py:262
  436.2 19.8 %copy-start.43 = (f32[3072]{0:T(1024)S(1)}, f32[3072]{0:T(1024)}, u32[]{:S(2)}) copy-start(f32[3072]{0:T(1024)} %get-tuple-element.72) | copy-start | bytes 36868
  436.2 19.8 %copy-start.48 = (f32[768]{0:T(1024)S(1)}, f32[768]{0:T(1024)}, u32[]{:S(2)}) copy-start(f32[768]{0:T(1024)} %get-tuple-element.13) | copy-start | bytes 9220
  436.2 19.8 %copy-start.47 = (f32[768]{0:T(1024)S(1)}, f32[768]{0:T(1024)}, u32[]{:S(2)}) copy-start(f32[768]{0:T(1024)} %get-tuple-element.18) | copy-start | bytes 9220
  436.2 19.8 %copy-start.38 = (f32[768]{0:T(1024)S(1)}, f32[768]{0:T(1024)}, u32[]{:S(2)}) copy-start(f32[768]{0:T(1024)} %get-tuple-element.40) | copy-start | bytes 9220
  436.2 19.8 %copy-start.26 = (f32[1200]{0:T(1024)S(1)}, f32[1200]{0:T(1024)}, u32[]{:S(2)}) copy-start(f32[1200]{0:T(1024)} %copy-done.25) | copy-start | bytes 14404
  436.2 19.8 %copy-start.30 = (f32[1200]{0:T(1024)S(1)}, f32[1200]{0:T(1024)}, u32[]{:S(2)}) copy-start(f32[1200]{0:T(1024)} %get-tuple-element.33) | copy-start | bytes 14404
  448.2 18.1 %all-to-all-start.3 = ((bf16[4,624,192]{1,2,0:T(8,128)(2,1)}), bf16[4,624,192]{1,2,0:T(8,128)(2,1)}, u32[]{:S(2)}, u32[]{:S(2)}) async-start(bf16[4,624,192]{1,2,0:T(8,128)(2,1)} %bitcast.31), calls=%async_computation.3 | async-start | bytes 1966080 | tf_op jit(solution)/shard_map/all_to_all | solution.py:262
  466.3 39.6 %all-to-all-start.7 = ((bf16[4,624,192]{1,2,0:T(8,128)(2,1)}), bf16[4,624,192]{1,2,0:T(8,128)(2,1)S(1)}, u32[]{:S(2)}, u32[]{:S(2)}) async-start(bf16[4,624,192]{1,2,0:T(8,128)(2,1)} %bitcast.213), calls=%async_computation.7 | async-start | bytes 1966080 | tf_op jit(solution)/shard_map/all_to_all | solution.py:262
  481.0 22.2 %collective-permute-start.6 = (bf16[576,768]{1,0:T(8,128)(2,1)}, bf16[576,768]{1,0:T(8,128)(2,1)S(1)}, u32[]{:S(2)}, u32[]{:S(2)}) collective-permute-start(bf16[576,768]{1,0:T(8,128)(2,1)} %slice.291), channel_id=1, source_target_pairs={{0,2},{1,3},{2,0},{3,1},{4,6},{5,7},{6,4},{7,5},{8,10},{9,11},{10,... | collective-permute-start | bytes 2654216 | tf_op jit(solution)/shard_map/ppermute | solution.py:175
  496.5 14.2 %copy-start.32 = (s32[4616]{0:T(1024)S(1)}, s32[4616]{0:T(1024)}, u32[]{:S(2)}) copy-start(s32[4616]{0:T(1024)} %get-tuple-element.45) | copy-start | bytes 55396
  505.9 30.7 %all-to-all-start.5 = ((bf16[8,72,768]{2,1,0:T(8,128)(2,1)}), bf16[8,72,768]{2,1,0:T(8,128)(2,1)S(1)}, u32[]{:S(2)}, u32[]{:S(2)}) async-start(bf16[8,72,768]{2,1,0:T(8,128)(2,1)} %bitcast.218), calls=%async_computation.5 | async-start | bytes 1769472 | tf_op jit(solution)/shard_map/all_to_all | solution.py:179
  510.6 172.1 %all-reduce.8.cloned.1.call-start = ((), (), s32[]{:S(2)}) async-start(), calls=%async_computation.14 | async-start | bytes 7077888 | tf_op jit(solution)/shard_map/psum | solution.py:250
  543.3 88.0 %all-to-all-start.6 = ((bf16[4,576,192]{1,2,0:T(8,128)(2,1)}), bf16[4,576,192]{1,2,0:T(8,128)(2,1)S(1)}, u32[]{:S(2)}, u32[]{:S(2)}) async-start(bf16[4,576,192]{1,2,0:T(8,128)(2,1)} %bitcast.43), calls=%async_computation.6 | async-start | bytes 1966080 | tf_op jit(solution)/shard_map/all_to_all | solution.py:262
  (30 other events, 139.2 us)
Sparse Core Ops, SparseCore 0:
  80.8 36.5 all-gather.7
  150.1 55.4 all-gather.9
  250.2 47.7 reduce-scatter.4
  350.1 46.8 reduce-scatter.2
  539.6 143.0 all-reduce.7
